TPU v7x, 32 devices: a whole 2x2x4 slice. The times are simulated.
32 devices in a mesh: seq: 4 (over y, x), grp: 2 (over core), wsh: 4 (over z).
Axes of the slice: x: 2, y: 2, z: 4, core: 2. Of those that a mesh axis runs over, the one named last changes fastest.
Arguments:
- hidden: bfloat16 [8, 1024, 1536], P(('grp', 'wsh'), 'seq'), may hold values from -6 to 6
- norm_gain: bfloat16 [1536], P('wsh'), may hold values from 0.5 to 1.5
- in_weight: bfloat16 [1536, 6448], P('wsh'), may hold values from -0.15625 to 0.15625
- conv_weight: bfloat16 [3328, 4], P('wsh'), may hold values from -3 to 3
- conv_bias: bfloat16 [3328], P('wsh'), may hold values from -3 to 3
- dt_bias: bfloat16 [48], P('wsh'), may hold values from -13 to -3
- a_log: bfloat16 [48], P('wsh'), may hold values from 0 to 2.7
- skip_gain: bfloat16 [48], P('wsh'), may hold values from 0.5 to 2
- gate_gain: bfloat16 [3072], P('wsh'), may hold values from 0.5 to 1.5
- out_weight: bfloat16 [3072, 1536], P('wsh'), may hold values from -0.109375 to 0.109375
- d_out: bfloat16 [8, 1024, 1536], P(('grp', 'wsh'), 'seq'), may hold values from -6 to 6
Outputs:
- layer_out: bfloat16 [8, 1024, 1536], P(('grp', 'wsh'), 'seq')
- d_hidden: bfloat16 [8, 1024, 1536], P(('grp', 'wsh'), 'seq')
- grad_norm_gain: float32 [1536], P('wsh')
- grad_in_weight: float32 [1536, 6448], P('wsh')
- grad_conv_weight: float32 [3328, 4], P('wsh')
- grad_conv_bias: float32 [3328], P('wsh')
- grad_dt_bias: float32 [48], P('wsh')
- grad_a_log: float32 [48], P('wsh')
- grad_skip_gain: float32 [48], P('wsh')
- grad_gate_gain: float32 [3072], P('wsh')
- grad_out_weight: float32 [3072, 1536], P('wsh')
All inputs are finite; a program needn't handle non-finite values.
Results may differ from a plain program's by a relative error of at most 0.0091.
Values may be sent and summed in bfloat16 or wider, within the bound.
No kernel may reach another device: no remote copies, remote signals or barrier semaphores. Data moves between devices by JAX's collectives and lax.ppermute only.
A program may use at most 320 MiB of HBM per device.

v0:
```python
import jax
import jax.numpy as jnp
from jax import lax
from jax.sharding import PartitionSpec as P

DI = 3072
KCONV = 4
QCH = 256
CONVC = 3328
epsilon = 1e-05
highest = lax.Precision.HIGHEST


def shifted(block, axis, distance):
    devices = range(lax.axis_size(axis))
    route = [(i - distance, i) for i in devices if i - distance in devices]
    return lax.ppermute(block, axis, route)


def rms_apply(values, gain_vec):
    inverse = lax.rsqrt(jnp.mean(values * values, axis=-1, keepdims=True) + epsilon)
    return values * inverse * gain_vec[None, :]


def gated_apply(mixer_out, gate_in, gain_vec):
    product = mixer_out * jax.nn.silu(gate_in)
    inverse = lax.rsqrt(jnp.mean(product * product, axis=-1, keepdims=True) + epsilon)
    return product * inverse * gain_vec[None, :]


def conv_apply(padded, weight, bias_vec):
    tap_count = weight.shape[1]
    row_count = padded.shape[0] - tap_count + 1
    summed = jnp.zeros((row_count, padded.shape[1]), jnp.float32) + bias_vec[None, :]
    for offset in range(tap_count):
        summed = summed + padded[offset : offset + row_count] * weight[:, offset][None, :]
    return jax.nn.silu(summed)


def ssd_apply(x_values, dt_raw, b_and_c, dt_bias, a_log, skip_gain):
    length, head_count = dt_raw.shape
    head_size = x_values.shape[1] // head_count
    state_count = b_and_c.shape[1] // 2
    block_count = length // QCH
    dt_value = jax.nn.softplus(dt_raw + dt_bias[None, :])
    log_rate = -jnp.exp(a_log)[None, :] * dt_value
    causal = (jnp.arange(QCH)[:, None] >= jnp.arange(QCH)[None, :]).astype(jnp.float32)
    x_blocks = x_values.reshape(block_count, QCH, head_count, head_size)
    dt_blocks = dt_value.reshape(block_count, QCH, head_count)
    rate_blocks = log_rate.reshape(block_count, QCH, head_count)
    b_blocks = b_and_c[:, :state_count].reshape(block_count, QCH, state_count)
    c_blocks = b_and_c[:, state_count:].reshape(block_count, QCH, state_count)

    def advance(carried, pieces):
        x_block, dt_block, rate_block, b_block, c_block = pieces
        cumulated = jnp.cumsum(rate_block, axis=0)
        gram_matrix = jnp.dot(c_block, b_block.T, precision=highest)
        spread = cumulated.T[:, :, None] - cumulated.T[:, None, :]
        mixing = (
            jnp.exp(spread * causal[None])
            * causal[None]
            * gram_matrix[None]
            * dt_block.T[:, None, :]
        )
        result = jnp.einsum("hts,shp->thp", mixing, x_block, precision=highest)
        result = (
            result
            + jnp.einsum("tn,hnp->thp", c_block, carried, precision=highest)
            * jnp.exp(cumulated)[:, :, None]
        )
        final_sum = cumulated[-1]
        tail_weight = jnp.exp(final_sum[None, :] - cumulated) * dt_block
        carried = carried * jnp.exp(final_sum)[:, None, None] + jnp.einsum(
            "sn,sh,shp->hnp", b_block, tail_weight, x_block, precision=highest
        )
        return (carried, result)

    initial = jnp.zeros((head_count, state_count, head_size), jnp.float32)
    _, outputs = lax.scan(advance, initial, (x_blocks, dt_blocks, rate_blocks, b_blocks, c_blocks))
    return (
        outputs.reshape(length, head_count * head_size)
        + x_values * jnp.repeat(skip_gain, head_size)[None, :]
    )


def reduce_grads(grads):
    shares = (
        lax.psum_scatter(grads[0], "wsh", scatter_dimension=0, tiled=True),
        lax.psum_scatter(grads[1], "wsh", scatter_dimension=0, tiled=True),
        lax.psum_scatter(grads[2], "wsh", scatter_dimension=0, tiled=True),
        lax.psum_scatter(grads[3], "wsh", scatter_dimension=0, tiled=True),
        lax.psum_scatter(grads[4], "wsh", scatter_dimension=0, tiled=True),
        lax.psum_scatter(grads[5], "wsh", scatter_dimension=0, tiled=True),
        lax.psum_scatter(grads[6], "wsh", scatter_dimension=0, tiled=True),
        lax.psum_scatter(grads[7], "wsh", scatter_dimension=0, tiled=True),
        lax.psum_scatter(grads[8], "wsh", scatter_dimension=0, tiled=True),
    )
    return lax.psum(
        (
            shares[0],
            shares[1],
            shares[2],
            shares[3],
            shares[4],
            shares[5],
            shares[6],
            shares[7],
            shares[8],
        ),
        ("seq", "grp"),
    )


def body(
    hidden,
    norm_gain,
    in_weight,
    conv_weight,
    conv_bias,
    dt_bias,
    a_log,
    skip_gain,
    gate_gain,
    out_weight,
    d_out,
):
    gathered = (
        lax.all_gather(norm_gain, "wsh", axis=0, tiled=True),
        lax.all_gather(in_weight, "wsh", axis=0, tiled=True),
        lax.all_gather(conv_weight, "wsh", axis=0, tiled=True),
        lax.all_gather(conv_bias, "wsh", axis=0, tiled=True),
        lax.all_gather(dt_bias, "wsh", axis=0, tiled=True),
        lax.all_gather(a_log, "wsh", axis=0, tiled=True),
        lax.all_gather(skip_gain, "wsh", axis=0, tiled=True),
    )
    full_norm, full_in, full_conv, full_cbias, full_dtb, full_alog, full_skip = gathered
    tokens_f = hidden[0].astype(jnp.float32)
    cotangent = d_out[0]
    normed_f, rms_back = jax.vjp(rms_apply, tokens_f, full_norm.astype(jnp.float32))
    normed = lax.optimization_barrier(normed_f.astype(jnp.bfloat16))
    projected = lax.optimization_barrier(
        jnp.dot(normed, full_in, preferred_element_type=jnp.float32).astype(jnp.bfloat16)
    )
    gate_part = projected[:, :DI]
    conv_input = projected[:, DI : DI + CONVC]
    dt_part = projected[:, DI + CONVC :]
    rim_rows = shifted(conv_input[conv_input.shape[0] - (KCONV - 1) :], "seq", 1)
    padded = jnp.concatenate([rim_rows, conv_input], axis=0).astype(jnp.float32)
    conved_f, conv_back = jax.vjp(
        conv_apply, padded, full_conv.astype(jnp.float32), full_cbias.astype(jnp.float32)
    )
    conved = lax.optimization_barrier(conved_f.astype(jnp.bfloat16))
    x_heads, dt_heads = (
        lax.all_to_all(conved[:, :DI], "seq", split_axis=1, concat_axis=0, tiled=True),
        lax.all_to_all(dt_part, "seq", split_axis=1, concat_axis=0, tiled=True),
    )
    bc_whole = lax.all_gather(conved[:, DI:], "seq", axis=0, tiled=True)
    local_heads = dt_heads.shape[1]
    head_start = lax.axis_index("seq") * local_heads
    bias_local = lax.dynamic_slice_in_dim(full_dtb.astype(jnp.float32), head_start, local_heads)
    alog_local = lax.dynamic_slice_in_dim(full_alog.astype(jnp.float32), head_start, local_heads)
    skip_local = lax.dynamic_slice_in_dim(full_skip.astype(jnp.float32), head_start, local_heads)
    x_float = x_heads.astype(jnp.float32)
    dt_float = dt_heads.astype(jnp.float32)
    bc_float = bc_whole.astype(jnp.float32)
    y_heads = ssd_apply(x_float, dt_float, bc_float, bias_local, alog_local, skip_local).astype(
        jnp.bfloat16
    )
    y_tokens = lax.all_to_all(y_heads, "seq", split_axis=0, concat_axis=1, tiled=True)
    full_gate, full_out = (
        lax.all_gather(gate_gain, "wsh", axis=0, tiled=True),
        lax.all_gather(out_weight, "wsh", axis=0, tiled=True),
    )
    gated_f, gate_back = jax.vjp(
        gated_apply,
        y_tokens.astype(jnp.float32),
        gate_part.astype(jnp.float32),
        full_gate.astype(jnp.float32),
    )
    gated = gated_f.astype(jnp.bfloat16)
    layer_out = (tokens_f + jnp.dot(gated, full_out, preferred_element_type=jnp.float32)).astype(
        jnp.bfloat16
    )
    grad_out = jnp.einsum("td,te->de", gated, cotangent, preferred_element_type=jnp.float32)
    d_gated = lax.dot_general(
        cotangent, full_out, (((1,), (1,)), ((), ())), preferred_element_type=jnp.float32
    )
    d_mixer, d_gate_part, grad_gate = gate_back(d_gated)
    d_y_heads = lax.all_to_all(
        d_mixer.astype(jnp.bfloat16), "seq", split_axis=1, concat_axis=0, tiled=True
    )
    _, ssd_back = jax.vjp(
        ssd_apply, x_float, dt_float, bc_float, bias_local, alog_local, skip_local
    )
    d_x, d_dt, d_bc_part, grad_dtb, grad_alog, grad_skip = ssd_back(d_y_heads.astype(jnp.float32))
    d_bc = lax.psum_scatter(d_bc_part, "seq", scatter_dimension=0, tiled=True)
    d_x_tokens, d_dt_tokens = (
        lax.all_to_all(d_x.astype(jnp.bfloat16), "seq", split_axis=0, concat_axis=1, tiled=True),
        lax.all_to_all(d_dt.astype(jnp.bfloat16), "seq", split_axis=0, concat_axis=1, tiled=True),
    )
    d_conved = jnp.concatenate([d_x_tokens.astype(jnp.float32), d_bc], axis=1)
    d_padded, grad_conv, grad_cbias = conv_back(d_conved)
    rim_grad = shifted(d_padded[: KCONV - 1].astype(jnp.bfloat16), "seq", -1).astype(jnp.float32)
    own_rows = conv_input.shape[0]
    d_conv_input = d_padded[KCONV - 1 :] + jnp.concatenate(
        [jnp.zeros((own_rows - (KCONV - 1), CONVC), jnp.float32), rim_grad], axis=0
    )
    d_projected = jnp.concatenate(
        [d_gate_part, d_conv_input, d_dt_tokens.astype(jnp.float32)], axis=1
    ).astype(jnp.bfloat16)
    grad_in = jnp.einsum("td,tp->dp", normed, d_projected, preferred_element_type=jnp.float32)
    d_normed = lax.dot_general(
        d_projected, full_in, (((1,), (1,)), ((), ())), preferred_element_type=jnp.float32
    )
    d_tokens, grad_norm = rms_back(d_normed)
    d_hidden = (cotangent.astype(jnp.float32) + d_tokens).astype(jnp.bfloat16)
    all_heads = full_dtb.shape[0]
    placed_dtb = lax.dynamic_update_slice_in_dim(
        jnp.zeros((all_heads,), jnp.float32), grad_dtb, head_start, 0
    )
    placed_alog = lax.dynamic_update_slice_in_dim(
        jnp.zeros((all_heads,), jnp.float32), grad_alog, head_start, 0
    )
    placed_skip = lax.dynamic_update_slice_in_dim(
        jnp.zeros((all_heads,), jnp.float32), grad_skip, head_start, 0
    )
    reduced = reduce_grads(
        (
            grad_norm,
            grad_in,
            grad_conv,
            grad_cbias,
            placed_dtb,
            placed_alog,
            placed_skip,
            grad_gate,
            grad_out,
        )
    )
    return (
        layer_out[None],
        d_hidden[None],
        reduced[0],
        reduced[1],
        reduced[2],
        reduced[3],
        reduced[4],
        reduced[5],
        reduced[6],
        reduced[7],
        reduced[8],
    )


def solution(mesh):
    placed = (
        P(("grp", "wsh"), "seq", None),
        P("wsh"),
        P("wsh", None),
        P("wsh", None),
        P("wsh"),
        P("wsh"),
        P("wsh"),
        P("wsh"),
        P("wsh"),
        P("wsh", None),
        P(("grp", "wsh"), "seq", None),
    )
    return jax.shard_map(
        body,
        mesh=mesh,
        in_specs=placed,
        out_specs=(
            P(("grp", "wsh"), "seq", None),
            P(("grp", "wsh"), "seq", None),
            P("wsh"),
            P("wsh", None),
            P("wsh", None),
            P("wsh"),
            P("wsh"),
            P("wsh"),
            P("wsh"),
            P("wsh"),
            P("wsh", None),
        ),
        check_vma=False,
    )
```

profile of v0, /device:TPU:0, one launch (start us, length us, event | category | flops | bytes accessed | tf_op | source)
XLA Modules:
  0.0 2245.3 jit_solution(12582450332125656297)
XLA Ops:
  9.0 13.6 all-gather
  22.7 13.5 all-gather.1
  37.5 312.8 %all-gather.6.cloned.1.call-done = bf16[1536,6448]{0,1:T(8,128)(2,1)} async-done(((bf16[384,6448]{0,1:T(8,128)(2,1)}), bf16[1536,6448]{0,1:T(8,128)(2,1)}) %all-gather.6.cloned.1.call-update) | async-done | bytes 19808272 | tf_op jit(solution)/shard_map/all_gather | solution.py:129
  350.3 10.3 convolution_convert_fusion
  370.2 10.7 all-reduce.25
  389.6 6.9 multiply_convert_fusion
  397.8 4.4 all-to-all-start.1
  404.4 26.2 %all_gather.36 = bf16[1024,256]{0,1:T(8,128)(2,1)S(1)} all-gather(bf16[256,256]{0,1:T(8,128)(2,1)S(1)} %slice.146), channel_id=1, replica_groups=mesh['seq'=4,'grp'=2,'wsh'=4] {'seq'}, dimensions={0}, use_global_device_ids=true | all-gather | bytes 655360 | tf_op jit(solution)/shard_map/all_gather | solution.py:157
  436.7 52.1 %while.86 = (s32[]{:T(128)}, f32[12,128,64]{1,2,0:T(8,128)}, f32[4,256,12,64]{1,3,2,0:T(8,128)}, f32[4,256,12]{1,2,0:T(8,128)}, f32[4,256,12]{1,2,0:T(8,128)S(1)...) while((s32[]{:T(128)}, f32[12,128,64]{1,2,0:T(8,128)}, ...), condition=%wide.region_4.5_spmd.clone.clone, body=%wide.region_1.4_spmd.clone.clone.sunk | while | flops 1313970176 | bytes 8233615 | solution.py:79
  444.2 4.7 fusion.259
  457.5 4.8 fusion.259
  470.7 4.7 fusion.259
  484.0 4.7 fusion.259
  492.7 4.5 all-to-all-start.2
  497.3 19.0 all-gather.2
  516.3 4.6 multiply_reduce_fusion.7
  521.5 8.7 multiply_reduce_fusion.4
  530.3 5.1 fusion.160
  535.4 4.3 all-to-all-start.3
  545.9 128.5 %while.87 = (s32[]{:T(128)}, f32[12,128,64]{1,2,0:T(8,128)}, f32[4,128,256]{1,2,0:T(8,128)}, f32[4,12,256,256]{3,2,1,0:T(8,128)}, f32[4,1,256,256]{3,2,1,0:T(8,1...) while((s32[]{:T(128)}, f32[12,128,64]{1,2,0:T(8,128)}, ...), condition=%wide.region_10.11_spmd.clone.clone, body=%wide.region_7.10_spmd.clone.clone.sunk | while | flops 709793792 | bytes 22214624 | solution.py:79
  572.1 5.3 multiply_dynamic-update-slice_fusion.3
  604.6 5.1 multiply_dynamic-update-slice_fusion.3
  636.9 5.1 multiply_dynamic-update-slice_fusion.3
  669.1 5.2 multiply_dynamic-update-slice_fusion.3
  682.6 290.8 %while.88 = (s32[]{:T(128)}, f32[12,128,64]{1,2,0:T(8,128)S(1)}, f32[4,256,12,64]{1,3,2,0:T(8,128)}, f32[4,256,12]{1,2,0:T(8,128)}, f32[4,256,12]{1,2,0:T(8,128)...) while((s32[]{:T(128)}, f32[12,128,64]{1,2,0:T(8,128)S(1)}, ...), condition=%wide.region_21.22_spmd.clone.clone, body=%wide.region_11.21_spmd.clone.clone.sunk | while | flops 2628807680 | bytes 29113356 | solution.py:79
  708.5 9.3 fusion.282
  750.1 5.3 fusion.281
  781.1 9.3 fusion.282
  822.7 5.3 fusion.281
  853.7 9.3 fusion.282
  895.3 5.2 fusion.281
  926.3 9.4 fusion.282
  968.0 5.2 fusion.281
  980.1 9.4 fusion.176
  992.9 24.3 %all_to_all.69 = bf16[4,256,768]{1,2,0:T(8,128)(2,1)S(1)} all-to-all(bf16[4,256,768]{1,2,0:T(8,128)(2,1)S(1)} %fusion.161), channel_id=1, replica_groups=mesh['seq'=4,'grp'=2,'wsh'=4] {'seq'}, dimensions={0} | all-to-all | bytes 3145728 | tf_op jit(solution)/shard_map/all_to_all | solution.py:198
  1019.2 12.2 multiply_reduce_fusion.3
  1033.9 4.2 pad_add_fusion
  1044.5 9.7 all_to_all.70
  1055.6 4.9 fusion.154
  1060.5 19.0 fusion.173
  1081.5 252.9 %reduce-scatter.11.cloned.1.call-done = f32[768,1536]{1,0:T(8,128)} async-done(((f32[3072,1536]{1,0:T(8,128)}), f32[768,1536]{1,0:T(8,128)}) %reduce-scatter.11.cloned.1.call-update) | async-done | bytes 4718608 | tf_op jit(solution)/shard_map/reduce_scatter | solution.py:96
  1334.4 651.6 %reduce-scatter.9.cloned.1.call-done = f32[384,6448]{0,1:T(8,128)} async-done(((f32[1536,6448]{0,1:T(8,128)}), f32[384,6448]{0,1:T(8,128)}) %reduce-scatter.9.cloned.1.call-update) | async-done | bytes 9904144 | tf_op jit(solution)/shard_map/reduce_scatter | solution.py:89
  1988.7 7.5 fusion.164
  1999.9 14.0 fusion.168
  2013.9 21.4 all-reduce.24
  2039.8 24.8 %all-reduce.22 = (f32[384]{0:T(512)}, f32[832,4]{0,1:T(4,128)}, f32[832]{0:T(1024)}, f32[12]{0:T(128)}, f32[12]{0:T(128)}, /*index=5*/f32[12]{0:T(128)}, f32[768]{0:T(1024)}) all-reduce(f32[384]{0:T(512)S(1)} %dynamic-slice.5, f32[832,4]{0,1:T(4,128)S(1)} %copy.193, ...), channel_id=1, replica_groups=mesh['seq'=4,'grp'=2,'wsh'=4] {'seq','grp'}, use_global_device_ids=true, to_apply=%region_26.27 | all-reduce | flops 5348 | bytes 42784 | tf_op jit(solution)/shard_map/psum | solution.py:98
  2064.6 163.0 %all-reduce.28.cloned.1.call-done = (f32[384,6448]{0,1:T(8,128)}, f32[768,1536]{1,0:T(8,128)}) async-done(((f32[384,6448]{0,1:T(8,128)}, f32[768,1536]{1,0:T(8,128)}), (f32[384,6448]{0,1:T(8,128)}, f32[768,1536]{1,0:T(8,128)})) %all-reduce.28.cloned.1.call-update) | async-done | bytes 14622736 | tf_op jit(solution)/shard_map/psum | solution.py:98
  2227.6 8.5 copy.389
  (596 shorter events, 454.9 us)
Async XLA Ops:
  7.2 15.5 copy-start.41
  7.2 343.1 %all-gather.6.cloned.1.call-start = ((), (), s32[]{:S(2)}) async-start(), calls=%async_computation.10 | async-start | bytes 24760320 | tf_op jit(solution)/shard_map/all_gather | solution.py:129
  7.9 513.5 %all-gather.8.cloned.1.call-start = ((), (), s32[]{:S(2)}) async-start(), calls=%async_computation.11 | async-start | bytes 11796480 | tf_op jit(solution)/shard_map/all_gather | solution.py:172
  8.9 13.7 copy-start.35
  9.0 351.7 %copy-start.37 = (f32[256]{0:T(256)}, f32[256]{0:T(256)S(1)}, u32[]{:S(2)}) copy-start(f32[256]{0:T(256)S(1)} %fusion.187) | copy-start | bytes 3076
  22.7 338.0 %copy-start.29 = (f32[1536]{0:T(1024)}, f32[1536]{0:T(1024)S(1)}, u32[]{:S(2)}) copy-start(f32[1536]{0:T(1024)S(1)} %reshape.483) | copy-start | bytes 18436
  37.5 329.9 %copy-start.46 = (u32[32]{0:T(128)S(1)}, u32[32]{0:T(128)}, u32[]{:S(2)}) copy-start(u32[32]{0:T(128)} %constant.226) | copy-start | bytes 388
  37.5 331.8 %copy-start.52 = (bf16[12]{0:T(256)(128)(2,1)S(1)}, bf16[12]{0:T(256)(128)(2,1)}, u32[]{:S(2)}) copy-start(bf16[12]{0:T(256)(128)(2,1)} %param.22) | copy-start | bytes 76
  37.5 332.0 %copy-start.53 = (bf16[12]{0:T(256)(128)(2,1)S(1)}, bf16[12]{0:T(256)(128)(2,1)}, u32[]{:S(2)}) copy-start(bf16[12]{0:T(256)(128)(2,1)} %param.23) | copy-start | bytes 76
  37.5 332.3 %copy-start.54 = (bf16[12]{0:T(256)(128)(2,1)S(1)}, bf16[12]{0:T(256)(128)(2,1)}, u32[]{:S(2)}) copy-start(bf16[12]{0:T(256)(128)(2,1)} %param.24) | copy-start | bytes 76
  37.5 332.5 %copy-start.47 = (bf16[832]{0:T(1024)(128)(2,1)S(1)}, bf16[832]{0:T(1024)(128)(2,1)}, u32[]{:S(2)}) copy-start(bf16[832]{0:T(1024)(128)(2,1)} %param.21) | copy-start | bytes 4996
  360.7 22.3 copy-start.6
  363.9 22.6 %collective-permute-start = (bf16[3,3328]{1,0:T(4,128)(2,1)S(1)}, bf16[3,3328]{1,0:T(4,128)(2,1)S(1)}, u32[]{:S(2)}, u32[]{:S(2)}) collective-permute-start(bf16[3,3328]{1,0:T(4,128)(2,1)S(1)} %copy.162), channel_id=1, source_target_pairs={{0,8},{8,16},{16,24},{1,9},{9,17},{17,25},{2,10},{10,18},{18,26},{... | collective-permute-start | bytes 59912 | tf_op jit(solution)/shard_map/ppermute | solution.py:17
  367.3 22.2 copy-start.21
  367.3 22.2 copy-start.23
  367.3 22.2 copy-start.25
  367.3 22.2 copy-start.27
  382.9 14.8 all-to-all-start
  397.8 35.0 %all-to-all-start.1 = ((bf16[256,4,768]{0,2,1:T(8,128)(2,1)}), bf16[256,4,768]{0,2,1:T(8,128)(2,1)}, u32[]{:S(2)}, u32[]{:S(2)}) async-start(bf16[256,4,768]{0,2,1:T(8,128)(2,1)} %bitcast.6), calls=%async_computation.1 | async-start | bytes 3145728 | tf_op jit(solution)/shard_map/all_to_all | solution.py:154
  492.7 23.6 %all-to-all-start.2 = ((bf16[4,256,768]{1,2,0:T(8,128)(2,1)}), bf16[4,256,768]{1,2,0:T(8,128)(2,1)}, u32[]{:S(2)}, u32[]{:S(2)}) async-start(bf16[4,256,768]{1,2,0:T(8,128)(2,1)} %fusion.162), calls=%async_computation.2 | async-start | bytes 3145728 | tf_op jit(solution)/shard_map/all_to_all | solution.py:169
  516.3 14.0 copy-start.15
  521.5 8.8 copy-start.31
  521.5 8.8 copy-start.40
  521.5 8.8 copy-start.1
  535.4 138.9 %all-to-all-start.3 = ((bf16[256,4,768]{0,2,1:T(8,128)(2,1)}), bf16[256,4,768]{0,2,1:T(8,128)(2,1)}, u32[]{:S(2)}, u32[]{:S(2)}) async-start(bf16[256,4,768]{0,2,1:T(8,128)(2,1)} %bitcast.595), calls=%async_computation.3 | async-start | bytes 3145728 | tf_op jit(solution)/shard_map/all_to_all | solution.py:189
  539.7 479.4 %reduce-scatter.7.cloned.1.call-start = ((), (), s32[]{:S(2)}) async-start(), calls=%async_computation.12 | async-start | bytes 1310720 | tf_op jit(solution)/shard_map/reduce_scatter | solution.py:196
  701.0 7.5 copy-start.14
  773.6 7.5 copy-start.14
  846.2 7.5 copy-start.14
  918.8 7.5 copy-start.14
  980.0 354.4 %reduce-scatter.11.cloned.1.call-start = ((), (), s32[]{:S(2)}) async-start(), calls=%async_computation.14 | async-start | bytes 23592960 | tf_op jit(solution)/shard_map/reduce_scatter | solution.py:96
  989.5 996.6 %reduce-scatter.9.cloned.1.call-start = ((), (), s32[]{:S(2)}) async-start(), calls=%async_computation.13 | async-start | bytes 49520640 | tf_op jit(solution)/shard_map/reduce_scatter | solution.py:89
  1019.2 12.2 copy-start.22
  1019.2 12.2 copy-start.24
  1019.2 12.2 copy-start.26
  1019.2 12.3 copy-start.28
  1033.8 10.4 copy-start.18
  1033.8 10.4 copy-start.19
  1033.8 10.4 copy-start.20
  1033.9 10.4 copy-start.43
  1033.9 10.4 copy-start.45
  1042.9 11.4 collective-permute-start.1
  1079.5 959.1 %reduce-scatter.13.cloned.1.call-start = ((), (), s32[]{:S(2)}) async-start(), calls=%async_computation.15 | async-start | bytes 2129920
  1081.4 1146.1 %all-reduce.28.cloned.1.call-start = ((), (), s32[]{:S(2)}) async-start(), calls=%async_computation.16 | async-start | bytes 29245440 | tf_op jit(solution)/shard_map/psum | solution.py:98
  1999.9 14.0 copy-start.34
  1999.9 35.8 %copy-start.36 = (f32[256]{0:T(256)S(1)}, f32[256]{0:T(256)}, u32[]{:S(2)}) copy-start(f32[256]{0:T(256)} %copy-done.35) | copy-start | bytes 3076
  1999.9 35.8 %copy-start.13 = (bf16[1,256,1536]{2,1,0:T(8,128)(2,1)S(1)}, bf16[1,256,1536]{2,1,0:T(8,128)(2,1)}, u32[]{:S(2)}) copy-start(bf16[1,256,1536]{2,1,0:T(8,128)(2,1)} %param.27) | copy-start | bytes 2359300
  2227.6 8.5 copy-start.9
  (29 other events, 105.4 us)
Sparse Core Ops, SparseCore 0:
  9.6 340.6 all-gather.5
  351.9 166.4 all-gather.7
  980.1 36.9 reduce-scatter.6
  1019.4 315.0 reduce-scatter.10
  1336.6 649.3 reduce-scatter.8
  1988.8 40.4 reduce-scatter.12
  2033.1 194.4 all-reduce.27
where the time goes:
time: 2260 us; the launch traced here: 2250 us
  waiting for transfers between devices  1380 us (61%)
  matrix products  257 us (11%)
  local copies, waits for them, and re-layouts  225 us (10%)
  other arithmetic  176 us (8%)
  blocking collectives  163 us (7%)
    reduce_scatter x1, waiting for transfers between devices, reduce_grads(): lax.psum_scatter(grads[1], 'wsh', scatter_dimension=0, tiled=True)  652 us
    all_gather x1, waiting for transfers between devices, body(): lax.all_gather(in_weight, 'wsh', axis=0, tiled=True)  313 us
    reduce_scatter x1, waiting for transfers between devices, reduce_grads(): lax.psum_scatter(grads[8], 'wsh', scatter_dimension=0, tiled=True)  253 us
    psum x1, waiting for transfers between devices, reduce_grads(): lax.psum((shares[0], shares[1], shares[2], shares[3], shares[4], shares[5...  163 us
    dot_general x12, matrix products, advance(): result = jnp.einsum('hts,shp->thp', mixing, x_block, precision=highest)  77.1 us
    another operation x42, other arithmetic  46.3 us
  transfers between devices with their start and end apart: 13, of which 4 were waited for; matrix products, arithmetic and copies ran while one was open for 14% of the time, Pallas kernels for 0%

commit v1 on v0

--- a/solution.py
+++ b/solution.py
@@ -9,6 +9,11 @@
 CONVC = 3328
 epsilon = 1e-05
 highest = lax.Precision.HIGHEST
+
+
+def one_after_other(array, first, second):
+    inner = lax.psum(array, first)
+    return lax.psum(inner, second)
 
 
 def shifted(block, axis, distance):
@@ -95,7 +100,7 @@
         lax.psum_scatter(grads[7], "wsh", scatter_dimension=0, tiled=True),
         lax.psum_scatter(grads[8], "wsh", scatter_dimension=0, tiled=True),
     )
-    return lax.psum(
+    return one_after_other(
         (
             shares[0],
             shares[1],
@@ -107,7 +112,8 @@
             shares[7],
             shares[8],
         ),
-        ("seq", "grp"),
+        "grp",
+        "seq",
     )
 
 

time: 2260 us -> 2420 us (1.071)
  waiting for transfers between devices: 1380 us -> 1530 us
    psum x1 -> x2, waiting for transfers between devices: 163 us -> 301 us  [the longest x1 245 us: one_after_other(): return lax.psum(inner, second)]
  transfers between devices with their start and end apart: 13 -> 14, of which waited for: 4 -> 6; matrix products, arithmetic and copies ran while one was open for 14% -> 14% of each run, Pallas kernels for 0% -> 0%
where the time goes in v1:
time: 2420 us; the launch traced here: 2410 us
  waiting for transfers between devices  1530 us (63%)
  matrix products  253 us (10%)
  local copies, waits for them, and re-layouts  239 us (10%)
  other arithmetic  180 us (7%)
  blocking collectives  155 us (6%)
    reduce_scatter x1, waiting for transfers between devices, reduce_grads(): lax.psum_scatter(grads[1], 'wsh', scatter_dimension=0, tiled=True)  652 us
    all_gather x1, waiting for transfers between devices, body(): lax.all_gather(in_weight, 'wsh', axis=0, tiled=True)  314 us
    reduce_scatter x1, waiting for transfers between devices, reduce_grads(): lax.psum_scatter(grads[8], 'wsh', scatter_dimension=0, tiled=True)  255 us
    psum x1, waiting for transfers between devices, one_after_other(): return lax.psum(inner, second)  245 us
    dot_general x12, matrix products, advance(): result = jnp.einsum('hts,shp->thp', mixing, x_block, precision=highest)  77 us
    another operation x73, local copies, waits for them, and re-layouts  59.2 us
    psum x1, waiting for transfers between devices, one_after_other(): inner = lax.psum(array, first)  56.5 us
    another operation x42, other arithmetic  52.6 us
  transfers between devices with their start and end apart: 14, of which 6 were waited for; matrix products, arithmetic and copies ran while one was open for 14% of the time, Pallas kernels for 0%

profile of v1, /device:TPU:0, one launch (start us, length us, event | category | flops | bytes accessed | tf_op | source)
XLA Modules:
  0.0 2405.4 jit_solution(1155109353591857116)
XLA Ops:
  9.0 13.6 all-gather
  22.7 13.5 all-gather.1
  36.7 313.6 %all-gather.6.cloned.1.call-done = bf16[1536,6448]{0,1:T(8,128)(2,1)} async-done(((bf16[384,6448]{0,1:T(8,128)(2,1)}), bf16[1536,6448]{0,1:T(8,128)(2,1)}) %all-gather.6.cloned.1.call-update) | async-done | bytes 19808272 | tf_op jit(solution)/shard_map/all_gather | solution.py:135
  350.3 11.5 convolution_convert_fusion
  370.8 10.2 all-reduce.27
  386.8 7.0 multiply_convert_fusion
  395.1 4.3 all-to-all-start.1
  401.2 26.7 %all_gather.36 = bf16[1024,256]{0,1:T(8,128)(2,1)S(1)} all-gather(bf16[256,256]{0,1:T(8,128)(2,1)S(1)} %slice.146), channel_id=1, replica_groups=mesh['seq'=4,'grp'=2,'wsh'=4] {'seq'}, dimensions={0}, use_global_device_ids=true | all-gather | bytes 655360 | tf_op jit(solution)/shard_map/all_gather | solution.py:163
  433.8 71.6 %while.86 = (s32[]{:T(128)}, f32[12,128,64]{1,2,0:T(8,128)S(1)}, f32[4,256,12,64]{1,3,2,0:T(8,128)}, f32[4,256,12]{1,2,0:T(8,128)}, f32[4,256,12]{1,2,0:T(8,128)...) while((s32[]{:T(128)}, f32[12,128,64]{1,2,0:T(8,128)S(1)}, ...), condition=%wide.region_4.5_spmd.clone.clone, body=%wide.region_1.4_spmd.clone.clone.sunk | while | flops 1313970176 | bytes 7889523 | solution.py:84
  447.0 4.7 fusion.259
  464.9 4.7 fusion.259
  482.8 4.7 fusion.259
  500.6 4.7 fusion.259
  509.3 4.5 all-to-all-start.2
  514.0 13.8 all-gather.2
  531.8 4.6 multiply_reduce_fusion.7
  537.0 8.6 multiply_reduce_fusion.4
  545.6 4.9 fusion.160
  550.6 4.4 all-to-all-start.3
  561.1 128.2 %while.87 = (s32[]{:T(128)}, f32[12,128,64]{1,2,0:T(8,128)}, f32[4,128,256]{1,2,0:T(8,128)}, f32[4,12,256,256]{3,2,1,0:T(8,128)}, f32[4,1,256,256]{3,2,1,0:T(8,1...) while((s32[]{:T(128)}, f32[12,128,64]{1,2,0:T(8,128)}, ...), condition=%wide.region_10.11_spmd.clone.clone, body=%wide.region_7.10_spmd.clone.clone.sunk | while | flops 709793792 | bytes 22214624 | solution.py:84
  587.2 5.1 multiply_dynamic-update-slice_fusion.3
  619.4 5.1 multiply_dynamic-update-slice_fusion.3
  651.7 5.2 multiply_dynamic-update-slice_fusion.3
  684.0 5.2 multiply_dynamic-update-slice_fusion.3
  697.5 300.1 %while.88 = (s32[]{:T(128)}, f32[12,128,64]{1,2,0:T(8,128)S(1)}, f32[4,256,12,64]{1,3,2,0:T(8,128)}, f32[4,256,12]{1,2,0:T(8,128)}, f32[4,256,12]{1,2,0:T(8,128)...) while((s32[]{:T(128)}, f32[12,128,64]{1,2,0:T(8,128)S(1)}, ...), condition=%wide.region_21.22_spmd.clone.clone, body=%wide.region_11.21_spmd.clone.clone.sunk | while | flops 2628807680 | bytes 29113356 | solution.py:84
  732.8 9.3 fusion.282
  774.4 5.3 fusion.281
  805.3 9.3 fusion.282
  847.0 5.3 fusion.281
  877.9 9.3 fusion.282
  919.6 5.3 fusion.281
  950.5 9.3 fusion.282
  992.1 5.3 fusion.281
  1004.2 9.5 fusion.176
  1017.3 25.5 %all_to_all.69 = bf16[4,256,768]{1,2,0:T(8,128)(2,1)S(1)} all-to-all(bf16[4,256,768]{1,2,0:T(8,128)(2,1)S(1)} %fusion.161), channel_id=1, replica_groups=mesh['seq'=4,'grp'=2,'wsh'=4] {'seq'}, dimensions={0} | all-to-all | bytes 3145728 | tf_op jit(solution)/shard_map/all_to_all | solution.py:204
  1044.8 12.5 multiply_reduce_fusion.3
  1059.8 4.2 pad_add_fusion
  1070.5 9.2 all_to_all.70
  1085.9 17.2 fusion.173
  1103.1 255.0 %reduce-scatter.11.cloned.1.call-done = f32[768,1536]{1,0:T(8,128)} async-done(((f32[3072,1536]{1,0:T(8,128)}), f32[768,1536]{1,0:T(8,128)}) %reduce-scatter.11.cloned.1.call-update) | async-done | bytes 4718608 | tf_op jit(solution)/shard_map/reduce_scatter | solution.py:101
  1358.2 651.6 %reduce-scatter.9.cloned.1.call-done = f32[384,6448]{0,1:T(8,128)} async-done(((f32[1536,6448]{0,1:T(8,128)}), f32[384,6448]{0,1:T(8,128)}) %reduce-scatter.9.cloned.1.call-update) | async-done | bytes 9904144 | tf_op jit(solution)/shard_map/reduce_scatter | solution.py:94
  2011.8 56.5 %all-reduce.33.cloned.1.call-done = (f32[384,6448]{0,1:T(8,128)}, f32[768,1536]{1,0:T(8,128)}) async-done(((f32[384,6448]{0,1:T(8,128)}, f32[768,1536]{1,0:T(8,128)}), (f32[384,6448]{0,1:T(8,128)}, f32[768,1536]{1,0:T(8,128)})) %all-reduce.33.cloned.1.call-update) | async-done | bytes 14622736 | tf_op jit(solution)/shard_map/psum | solution.py:15
  2070.9 7.4 fusion.164
  2081.8 13.9 fusion.168
  2095.7 21.0 all-reduce.22
  2124.8 18.2 all-reduce.23
  2142.9 244.7 %all-reduce.31.cloned.1.call-done = (f32[384,6448]{0,1:T(8,128)}, f32[768,1536]{1,0:T(8,128)}) async-done(((f32[384,6448]{0,1:T(8,128)}, f32[768,1536]{1,0:T(8,128)}), (f32[384,6448]{0,1:T(8,128)}, f32[768,1536]{1,0:T(8,128)})) %all-reduce.31.cloned.1.call-update) | async-done | bytes 14622736 | tf_op jit(solution)/shard_map/psum | solution.py:16
  2387.6 8.5 copy.391
  (594 shorter events, 481.7 us)
Async XLA Ops:
  7.2 15.5 copy-start.40
  7.2 343.1 %all-gather.6.cloned.1.call-start = ((), (), s32[]{:S(2)}) async-start(), calls=%async_computation.10 | async-start | bytes 24760320 | tf_op jit(solution)/shard_map/all_gather | solution.py:135
  7.9 529.0 %all-gather.8.cloned.1.call-start = ((), (), s32[]{:S(2)}) async-start(), calls=%async_computation.11 | async-start | bytes 11796480 | tf_op jit(solution)/shard_map/all_gather | solution.py:178
  8.9 13.7 copy-start.34
  9.0 352.8 %copy-start.36 = (f32[256]{0:T(256)}, f32[256]{0:T(256)S(1)}, u32[]{:S(2)}) copy-start(f32[256]{0:T(256)S(1)} %fusion.187) | copy-start | bytes 3076
  22.7 339.2 %copy-start.28 = (f32[1536]{0:T(1024)}, f32[1536]{0:T(1024)S(1)}, u32[]{:S(2)}) copy-start(f32[1536]{0:T(1024)S(1)} %reshape.483) | copy-start | bytes 18436
  36.6 325.2 %copy-start.11 = (bf16[256,1536]{1,0:T(8,128)(2,1)}, bf16[256,1536]{1,0:T(8,128)(2,1)S(1)}, u32[]{:S(2)}) copy-start(bf16[256,1536]{1,0:T(8,128)(2,1)S(1)} %fusion.167) | copy-start | bytes 2359300
  36.6 331.3 %copy-start.45 = (u32[32]{0:T(128)S(1)}, u32[32]{0:T(128)}, u32[]{:S(2)}) copy-start(u32[32]{0:T(128)} %constant.226) | copy-start | bytes 388
  36.6 333.2 %copy-start.51 = (bf16[12]{0:T(256)(128)(2,1)S(1)}, bf16[12]{0:T(256)(128)(2,1)}, u32[]{:S(2)}) copy-start(bf16[12]{0:T(256)(128)(2,1)} %param.22) | copy-start | bytes 76
  36.6 333.4 %copy-start.52 = (bf16[12]{0:T(256)(128)(2,1)S(1)}, bf16[12]{0:T(256)(128)(2,1)}, u32[]{:S(2)}) copy-start(bf16[12]{0:T(256)(128)(2,1)} %param.23) | copy-start | bytes 76
  36.6 333.6 %copy-start.53 = (bf16[12]{0:T(256)(128)(2,1)S(1)}, bf16[12]{0:T(256)(128)(2,1)}, u32[]{:S(2)}) copy-start(bf16[12]{0:T(256)(128)(2,1)} %param.24) | copy-start | bytes 76
  36.7 333.9 %copy-start.46 = (bf16[832]{0:T(1024)(128)(2,1)S(1)}, bf16[832]{0:T(1024)(128)(2,1)}, u32[]{:S(2)}) copy-start(bf16[832]{0:T(1024)(128)(2,1)} %param.21) | copy-start | bytes 4996
  363.8 17.2 slice-start
  363.8 21.9 slice-start.1
  364.2 21.0 collective-permute-start
  367.8 19.0 copy-start.20
  367.8 19.0 copy-start.22
  367.8 19.0 copy-start.24
  367.8 19.0 copy-start.26
  381.6 13.4 all-to-all-start
  395.1 33.0 %copy-start.16 = (bf16[256,4,12]{0,2,1:T(8,128)(2,1)}, bf16[256,4,12]{0,2,1:T(8,128)(2,1)S(1)}, u32[]{:S(2)}) copy-start(bf16[256,4,12]{0,2,1:T(8,128)(2,1)S(1)} %all-to-all-done) | copy-start | bytes 73732
  395.1 35.0 %all-to-all-start.1 = ((bf16[256,4,768]{0,2,1:T(8,128)(2,1)}), bf16[256,4,768]{0,2,1:T(8,128)(2,1)}, u32[]{:S(2)}, u32[]{:S(2)}) async-start(bf16[256,4,768]{0,2,1:T(8,128)(2,1)} %bitcast.595), calls=%async_computation.1 | async-start | bytes 3145728 | tf_op jit(solution)/shard_map/all_to_all | solution.py:160
  399.4 30.6 %copy-start.49 = (f32[48]{0:T(128)}, f32[48]{0:T(128)S(1)}, u32[]{:S(2)}) copy-start(f32[48]{0:T(128)S(1)} %convert_element_type.162) | copy-start | bytes 580
  399.5 30.6 %copy-start.41 = (f32[12]{0:T(128)}, f32[12]{0:T(128)S(1)}, u32[]{:S(2)}) copy-start(f32[12]{0:T(128)S(1)} %dynamic_slice.266) | copy-start | bytes 148
  400.4 29.7 %copy-start.43 = (f32[12]{0:T(128)}, f32[12]{0:T(128)S(1)}, u32[]{:S(2)}) copy-start(f32[12]{0:T(128)S(1)} %fusion.189) | copy-start | bytes 148
  509.3 22.5 all-to-all-start.2
  527.8 17.8 copy-start.13
  537.0 8.6 copy-start.30
  537.0 8.6 copy-start.1
  550.6 138.7 %all-to-all-start.3 = ((bf16[256,4,768]{0,2,1:T(8,128)(2,1)}), bf16[256,4,768]{0,2,1:T(8,128)(2,1)}, u32[]{:S(2)}, u32[]{:S(2)}) async-start(bf16[256,4,768]{0,2,1:T(8,128)(2,1)} %bitcast.596), calls=%async_computation.3 | async-start | bytes 3145728 | tf_op jit(solution)/shard_map/all_to_all | solution.py:195
  554.9 489.9 %reduce-scatter.7.cloned.1.call-start = ((), (), s32[]{:S(2)}) async-start(), calls=%async_computation.12 | async-start | bytes 1310720 | tf_op jit(solution)/shard_map/reduce_scatter | solution.py:202
  1004.2 354.0 %reduce-scatter.11.cloned.1.call-start = ((), (), s32[]{:S(2)}) async-start(), calls=%async_computation.14 | async-start | bytes 23592960 | tf_op jit(solution)/shard_map/reduce_scatter | solution.py:101
  1013.7 996.1 %reduce-scatter.9.cloned.1.call-start = ((), (), s32[]{:S(2)}) async-start(), calls=%async_computation.13 | async-start | bytes 49520640 | tf_op jit(solution)/shard_map/reduce_scatter | solution.py:94
  1044.8 12.5 copy-start.21
  1044.8 12.6 copy-start.23
  1044.8 12.6 copy-start.25
  1044.8 12.6 copy-start.27
  1059.8 10.4 copy-start.17
  1059.8 10.4 copy-start.18
  1059.8 10.4 copy-start.19
  1059.8 10.4 copy-start.42
  1059.8 10.4 copy-start.44
  1068.9 10.8 collective-permute-start.1
  1103.1 965.2 %all-reduce.33.cloned.1.call-start = ((), (), s32[]{:S(2)}) async-start(), calls=%async_computation.17 | async-start | bytes 29245440 | tf_op jit(solution)/shard_map/psum | solution.py:15
  2009.8 110.3 %reduce-scatter.13.cloned.1.call-start = ((), (), s32[]{:S(2)}) async-start(), calls=%async_computation.15 | async-start | bytes 2129920
  2011.8 375.9 %all-reduce.31.cloned.1.call-start = ((), (), s32[]{:S(2)}) async-start(), calls=%async_computation.16 | async-start | bytes 29245440 | tf_op jit(solution)/shard_map/psum | solution.py:16
  2081.7 13.9 copy-start.33
  2081.7 35.4 %copy-start.35 = (f32[256]{0:T(256)S(1)}, f32[256]{0:T(256)}, u32[]{:S(2)}) copy-start(f32[256]{0:T(256)} %copy-done.34) | copy-start | bytes 3076
  (28 other events, 140.1 us)
Sparse Core Ops, SparseCore 0:
  9.6 340.6 all-gather.5
  351.9 166.2 all-gather.7
  1004.3 38.3 reduce-scatter.6
  1044.8 313.2 reduce-scatter.10
  1360.4 649.3 reduce-scatter.8
  2012.2 56.0 all-reduce.32
  2071.2 39.5 reduce-scatter.12
  2114.5 273.0 all-reduce.30
